TPU v7x, 32 devices: a whole 2x2x4 slice. The times are simulated.
32 devices in a mesh: comp: 8 (over y, x, core), tile: 4 (over z).
Axes of the slice: x: 2, y: 2, z: 4, core: 2. Of those that a mesh axis runs over, the one named last changes fastest.
Arguments:
- atm_state: float32 [128, 128, 512], P(None, 'comp', 'tile'), may hold values from -6 to 6
- ocean_state: float32 [48, 128, 512], P(None, 'comp', 'tile'), may hold values from -6 to 6
- atm_rate: float32 [128], replicated, may hold values from 0.02 to 0.24
- ocean_rate: float32 [48], replicated, may hold values from 0.02 to 0.24
- ocean_mask: int32 [128, 4], P('comp', 'tile'), may hold values 0 or 1
- remap_weight: bfloat16 [8, 192, 128, 128], P('comp', 'tile'), may hold values from -0.5 to 0.5
- pair_src: int32 [8, 192], P('comp', 'tile'), may hold values from 0 to 63, as said below
- pair_tgt: int32 [8, 192], P('comp', 'tile'), may hold values from 0 to 63, as said below
- pair_count: int32 [8, 4], P('comp', 'tile'), may hold values from 24 to 48, as said below
Outputs:
- atm_next: float32 [128, 128, 512], P(None, 'comp', 'tile')
- ocean_next: float32 [48, 128, 512], P(None, 'comp', 'tile')
Inputs may be any that keep to these rules, and one draw needn't show every extreme that they name: `pair_src`: entry d * 48 + j of row b names atmosphere tile e * 16 + y of band b. Among the first pair_count[b, d] entries of device d at most 13 have the same e, and every device has 13 live entries with one same e. `pair_tgt`: entry d * 48 + j of row b names ocean tile e * 16 + y of band b. Among the first pair_count[b, d] entries of device d at most 13 have the same e, and every device has 13 live entries with one same e. `pair_count`: each row b has some device with 48 live slots.
All inputs are finite; a program needn't handle non-finite values. No bound on the sum of `ocean_mask` on one device may be relied on, other than what follows from the above.
Results may differ from a plain program's by a relative error of at most 0.002.
Values may be sent and summed in bfloat16 or wider, within the bound.
No kernel may reach another device: no remote copies, remote signals or barrier semaphores. Data moves between devices by JAX's collectives and lax.ppermute only.
A program may use at most 64 MiB of HBM per device.

v0:
```python
import jax
import jax.numpy as jnp
from jax import lax
from jax.sharding import PartitionSpec as P

SURF = 8


def padded_2(block, sides, width):
    for axis, dim in sides:
        count = lax.axis_size(axis)
        forward = [(i, i + 1) for i in range(count - 1)]
        forward.append((count - 1, 0))
        backward = [(target, source) for source, target in forward]
        low = lax.ppermute(
            lax.slice_in_dim(block, block.shape[dim] - width, None, axis=dim), axis, forward
        )
        high = lax.ppermute(lax.slice_in_dim(block, 0, width, axis=dim), axis, backward)
        block = jnp.concatenate([low, block, high], axis=dim)
    return block


def relax(padded, spread):
    center = padded[:, 1:-1, 1:-1]
    beside_all = (
        padded[:, 2:, 1:-1] + padded[:, :-2, 1:-1] + padded[:, 1:-1, 2:] + padded[:, 1:-1, :-2]
    )
    return center + spread[:, None, None] * (beside_all - 4.0 * center)


def ghosts(padded, width):
    row_total = padded.shape[1]
    row_index = jnp.arange(row_total)
    position = lax.axis_index("comp")
    at_first = jnp.logical_and(row_index < width, position == 0)
    at_last = jnp.logical_and(row_index >= row_total - width, position == lax.axis_size("comp") - 1)
    retain = jnp.logical_not(jnp.logical_or(at_first, at_last)).astype(jnp.float32)
    return padded * retain[None, :, None]


def shards(
    atm_state,
    ocean_state,
    atm_rate,
    ocean_rate,
    ocean_mask,
    remap_weight,
    pair_src,
    pair_tgt,
    pair_count,
):
    atm_rows = atm_state.shape[1]
    ocean_rows = ocean_state.shape[1]
    cell_total = atm_state.shape[2]
    pair_total = pair_src.shape[1]
    wet_rows = ocean_mask[:, 0].astype(jnp.float32)
    atm_source = atm_state[:SURF].astype(jnp.bfloat16)
    ocean_source = (ocean_state[:SURF] * wet_rows[None, :, None]).astype(jnp.bfloat16)
    atm_band, ocean_band = (
        lax.all_gather(atm_source, "tile", axis=1, tiled=True),
        lax.all_gather(ocean_source, "tile", axis=1, tiled=True),
    )
    anchor = pair_src[0]
    target = pair_tgt[0]
    active = jnp.arange(pair_total) < pair_count[0, 0]
    active_float = active.astype(jnp.float32)[:, None, None]
    weights = remap_weight[0]
    forward = (
        jnp.einsum(
            "fpt,pts->pfs",
            jnp.take(atm_band, anchor, axis=1),
            weights,
            preferred_element_type=jnp.float32,
        )
        * active_float
    )
    reverse = (
        jnp.einsum(
            "fps,pts->pft",
            jnp.take(ocean_band, target, axis=1),
            weights,
            preferred_element_type=jnp.float32,
        )
        * active_float
    )
    band_rows = atm_rows + ocean_rows
    ahead_codes = jnp.where(
        active, target // ocean_rows * band_rows + atm_rows + target % ocean_rows, -1
    )
    back_codes = jnp.where(active, anchor // atm_rows * band_rows + anchor % atm_rows, -1)
    ahead_flat = forward.reshape(pair_total, -1)
    back_flat = reverse.reshape(pair_total, -1)
    row_codes = jnp.arange(band_rows * lax.axis_size("tile"))
    ahead_hot = (row_codes[:, None] == ahead_codes[None, :]).astype(jnp.float32)
    back_hot = (row_codes[:, None] == back_codes[None, :]).astype(jnp.float32)
    summed = lax.psum_scatter(
        jnp.dot(
            ahead_hot,
            ahead_flat,
            precision=lax.Precision.HIGHEST,
            preferred_element_type=jnp.float32,
        )
        + jnp.dot(
            back_hot, back_flat, precision=lax.Precision.HIGHEST, preferred_element_type=jnp.float32
        ),
        "tile",
        scatter_dimension=0,
        tiled=True,
    )
    atm_force = summed[:atm_rows].reshape(atm_rows, SURF, cell_total)
    ocean_force = summed[atm_rows:].reshape(ocean_rows, SURF, cell_total)
    atm_padded = ghosts(padded_2(atm_state, (("comp", 1), ("tile", 2)), 2), 2)
    atm_stepped = relax(ghosts(relax(atm_padded, atm_rate), 1), atm_rate)
    ocean_padded = ghosts(padded_2(ocean_state, (("comp", 1), ("tile", 2)), 2), 2)
    ocean_stepped = relax(ghosts(relax(ocean_padded, ocean_rate), 1), ocean_rate)
    atm_next = atm_stepped.at[:SURF].add(jnp.transpose(atm_force, (1, 0, 2)))
    ocean_next = ocean_stepped.at[:SURF].add(
        jnp.transpose(ocean_force, (1, 0, 2)) * wet_rows[None, :, None]
    )
    return (atm_next, ocean_next)


def solution(mesh):
    return jax.shard_map(
        shards,
        mesh=mesh,
        in_specs=(
            P(None, "comp", "tile"),
            P(None, "comp", "tile"),
            P(),
            P(),
            P("comp", "tile"),
            P("comp", "tile", None, None),
            P("comp", "tile"),
            P("comp", "tile"),
            P("comp", "tile"),
        ),
        out_specs=(P(None, "comp", "tile"), P(None, "comp", "tile")),
        check_vma=False,
    )
```

profile of v0, /device:TPU:0, one launch (start us, length us, event | category | flops | bytes accessed | tf_op | source)
XLA Modules:
  0.0 102.0 jit_solution(3758282511293976926)
XLA Ops:
  7.3 2.0 %copy.67 = f32[128,16,128]{0,1,2:T(8,128)S(1)} copy(f32[128,16,128]{2,1,0:T(8,128)} %param.15) | data formatting | bytes 2097152 | tf_op args[0]
  9.2 0.8 fusion.48
  10.1 0.5 collective-permute-start
  10.6 2.9 %collective-permute-start.1 = (f32[128,2,128]{0,1,2:T(2,128)}, f32[128,2,128]{0,1,2:T(2,128)}, u32[]{:S(2)}, u32[]{:S(2)}) collective-permute-start(f32[128,2,128]{0,1,2:T(2,128)} %get-tuple-element.38), channel_id=1, source_target_pairs={{4,0},{8,4},{12,8},{16,12},{20,16},{24,20},{28,24},{0,28},{5,1},{9... | collective-permute-start | bytes 393224 | tf_op jit(solution)/shard_map/ppermute | solution.py:18
  13.4 0.8 slice.198
  15.0 14.4 %all_gather.6 = bf16[8,64,128]{2,0,1:T(8,128)(2,1)S(1)} all-gather(bf16[8,16,128]{2,0,1:T(8,128)(2,1)S(1)} %copy.100), channel_id=1, replica_groups=mesh['comp'=8,'tile'=4] {'tile'}, dimensions={1}, use_global_device_ids=true | all-gather | bytes 163840 | tf_op jit(solution)/shard_map/all_gather | solution.py:60
  29.4 0.6 fusion.43
  29.9 0.1 copy.74
  30.1 0.7 copy-done.2
  30.9 14.3 %all_gather.7 = bf16[8,64,128]{2,0,1:T(8,128)(2,1)} all-gather(bf16[8,16,128]{2,0,1:T(8,128)(2,1)S(1)} %fusion.36), channel_id=1, replica_groups=mesh['comp'=8,'tile'=4] {'tile'}, dimensions={1}, use_global_device_ids=true | all-gather | bytes 163840 | tf_op jit(solution)/shard_map/all_gather | solution.py:61
  45.2 0.6 fusion.44
  45.8 0.6 gather_fusion
  46.4 0.6 fusion.8
  47.0 0.4 fusion.26
  47.4 2.1 %gather_fusion.1 = bf16[48,8,128]{2,1,0:T(8,128)(2,1)} fusion(bf16[8,64,128]{2,0,1:T(8,128)(2,1)} %all_gather.7, s32[1024]{0:T(1024)S(1)} %pad_clamp_fusion), kind=kCustom, calls=%fused_computation.1.clone | custom fusion | bytes 196800 | tf_op jit(solution)/shard_map/jit(_take)/gather | solution.py:80
  49.6 1.8 %fusion.11 = f32[48,8,128]{2,1,0:T(8,128)S(1)} fusion(bf16[1,48,128,128]{3,2,1,0:T(8,128)(2,1)S(1)} %copy-done, bf16[48,8,128]{2,1,0:T(8,128)(2,1)} %gather_fusion.1, f32[48]{0:T(128)S(1)} %compare_convert_fusion, pred[48]{0:T(512)(128)(4,1)S(1)} %compare_and_fusion), kind=kOutput, calls=%fused_computation.17 | convolution fusion | flops 12681216 | bytes 1868016 | tf_op jit(solution)/shard_map/fps,pts->pft/dot_general | solution.py:78
  51.4 1.9 %convolution_add_fusion = f32[128,1024]{1,0:T(8,128)} fusion(f32[128,1024]{1,0:T(8,128)S(1)} %fusion.26, f32[6,8,8,128]{3,2,1,0:T(8,128)S(1)} %bitcast.52, s32[48]{0:T(128)} %fusion.44), kind=kOutput, calls=%fused_computation.15 | convolution fusion | flops 75634688 | bytes 1245376 | tf_op jit(solution)/shard_map/dot_general | solution.py:103
  53.3 1.4 %fusion.50 = (f32[48,2,128]{2,0,1:T(8,128)}, f32[48,2,128]{2,0,1:T(8,128)S(1)}) fusion(f32[48,16,128]{2,0,1:T(8,128)} %copy-done.2), kind=kLoop, calls=%fused_computation.98 | loop fusion | bytes 196608 | tf_op jit(solution)/shard_map/slice | solution.py:18
  54.8 2.6 %collective-permute-start.5 = (f32[48,2,128]{2,0,1:T(8,128)}, f32[48,2,128]{2,0,1:T(8,128)}, u32[]{:S(2)}, u32[]{:S(2)}) collective-permute-start(f32[48,2,128]{2,0,1:T(8,128)} %get-tuple-element.41), channel_id=1, source_target_pairs={{4,0},{8,4},{12,8},{16,12},{20,16},{24,20},{28,24},{0,28},{5,1},{9... | collective-permute-start | bytes 147464 | tf_op jit(solution)/shard_map/ppermute | solution.py:18
  57.4 1.9 %collective-permute-done.4 = f32[48,2,128]{2,0,1:T(8,128)} collective-permute-done((f32[48,2,128]{2,0,1:T(8,128)S(1)}, f32[48,2,128]{2,0,1:T(8,128)}, u32[]{:S(2)}, u32[]{:S(2)}) %collective-permute-start.4) | collective-permute-done | bytes 49184 | tf_op jit(solution)/shard_map/ppermute | solution.py:15
  59.3 0.8 constant_dynamic-update-slice_fusion.2
  60.2 0.8 constant_dynamic-update-slice_fusion
  61.0 1.1 %fusion.49 = (f32[48,20,2]{2,0,1:T(8,128)}, f32[48,20,2]{2,0,1:T(8,128)}) fusion(f32[48,20,128]{2,0,1:T(8,128)S(1)} %constant_dynamic-update-slice_fusion), kind=kLoop, calls=%fused_computation.97 | loop fusion | bytes 30720 | tf_op jit(solution)/shard_map/slice | solution.py:16
  62.1 1.3 %copy.79 = f32[48,20,2]{0,1,2:T(8,128)S(1)} copy(f32[48,20,2]{2,0,1:T(8,128)} %get-tuple-element.39) | data formatting | bytes 15360 | tf_op jit(solution)/shard_map/slice | solution.py:16
  63.3 1.5 %collective-permute-start.6 = (f32[48,20,2]{0,1,2:T(8,128)S(1)}, f32[48,20,2]{0,1,2:T(8,128)S(1)}, u32[]{:S(2)}, u32[]{:S(2)}) collective-permute-start(f32[48,20,2]{0,1,2:T(8,128)S(1)} %copy.79), channel_id=1, source_target_pairs={{0,1},{1,2},{2,3},{3,0},{4,5},{5,6},{6,7},{7,4},{8,9},{9,10},{10,1... | collective-permute-start | bytes 23048 | tf_op jit(solution)/shard_map/ppermute | solution.py:15
  64.9 1.3 %copy.80 = f32[48,20,2]{0,1,2:T(8,128)S(1)} copy(f32[48,20,2]{2,0,1:T(8,128)} %get-tuple-element.40) | data formatting | bytes 15360 | tf_op jit(solution)/shard_map/slice | solution.py:18
  66.2 2.4 %collective-permute-start.7 = (f32[48,20,2]{0,1,2:T(8,128)S(1)}, f32[48,20,2]{0,1,2:T(8,128)S(1)}, u32[]{:S(2)}, u32[]{:S(2)}) collective-permute-start(f32[48,20,2]{0,1,2:T(8,128)S(1)} %copy.80), channel_id=1, source_target_pairs={{1,0},{2,1},{3,2},{0,3},{5,4},{6,5},{7,6},{4,7},{9,8},{10,9},{11,1... | collective-permute-start | bytes 23048 | tf_op jit(solution)/shard_map/ppermute | solution.py:18
  68.5 0.8 collective-permute-done.6
  69.4 1.0 %copy.81 = f32[48,20,2]{2,0,1:T(8,128)} copy(f32[48,20,2]{0,1,2:T(8,128)S(1)} %collective-permute-done.6) | data formatting | bytes 15360 | tf_op jit(solution)/shard_map/ppermute | solution.py:15
  70.5 1.0 %copy.82 = f32[48,20,2]{2,0,1:T(8,128)} copy(f32[48,20,2]{0,1,2:T(8,128)S(1)} %collective-permute-done.7) | data formatting | bytes 15360 | tf_op jit(solution)/shard_map/ppermute | solution.py:18
  71.5 1.6 %maximum_multiply_fusion.1 = f32[48,20,132]{2,0,1:T(8,128)S(1)} fusion(f32[48,20,2]{2,0,1:T(8,128)} %copy.82, f32[48,20,128]{2,0,1:T(8,128)S(1)} %constant_dynamic-update-slice_fusion, f32[48,20,2]{2,0,1:T(8,128)} %copy.81, f32[20]{0:T(128)S(1)} %not_convert_fusion.1), kind=kLoop, calls=%fused_computation.25 | loop fusion | flops 380160 | bytes 1013840 | tf_op jit(solution)/shard_map/mul | solution.py:38
  73.1 1.0 fusion.20
  74.2 1.2 %pad_maximum_fusion = f32[128,20,128]{0,1,2:T(8,128)S(1)} fusion(f32[128,2,128]{0,1,2:T(2,128)} %collective-permute-done.1, f32[128,16,128]{0,1,2:T(8,128)S(1)} %copy.67, f32[128,2,128]{0,1,2:T(2,128)} %collective-permute-done), kind=kLoop, calls=%fused_computation.2 | loop fusion | flops 655360 | bytes 2621440 | tf_op jit(solution)/shard_map/concatenate | solution.py:19
  75.4 1.3 %collective-permute-start.2 = (f32[128,20,2]{0,1,2:T(8,128)S(1)}, f32[128,20,2]{0,1,2:T(8,128)S(1)}, u32[]{:S(2)}, u32[]{:S(2)}) collective-permute-start(f32[128,20,2]{0,1,2:T(8,128)S(1)} %get-tuple-element.35), channel_id=1, source_target_pairs={{0,1},{1,2},{2,3},{3,0},{4,5},{5,6},{6,7},{7,4},{8,9},{9,10},{10,1... | collective-permute-start | bytes 61448 | tf_op jit(solution)/shard_map/ppermute | solution.py:15
  76.7 3.1 %collective-permute-start.3 = (f32[128,20,2]{0,1,2:T(8,128)S(1)}, f32[128,20,2]{0,1,2:T(8,128)S(1)}, u32[]{:S(2)}, u32[]{:S(2)}) collective-permute-start(f32[128,20,2]{0,1,2:T(8,128)S(1)} %get-tuple-element.36), channel_id=1, source_target_pairs={{1,0},{2,1},{3,2},{0,3},{5,4},{6,5},{7,6},{4,7},{9,8},{10,9},{11,1... | collective-permute-start | bytes 61448 | tf_op jit(solution)/shard_map/ppermute | solution.py:18
  79.8 0.5 fusion.23
  80.3 0.3 copy.71
  80.5 1.0 collective-permute-done.2
  81.6 0.2 maximum_multiply_fusion
  81.8 0.4 copy-done.4
  82.2 0.5 fusion.7
  82.7 0.4 fusion.16
  83.1 0.9 slice_bitcast_fusion
  84.0 1.3 %copy.75 = f32[16,8,128]{1,2,0:T(8,128)} copy(f32[16,8,128]{2,1,0:T(8,128)S(1)} %bitcast.54) | data formatting | bytes 131072 | tf_op jit(solution)/shard_map/reshape | solution.py:110
  85.4 2.3 %slice_add_fusion.3 = f32[8,16,128]{0,2,1:T(8,128)} fusion(f32[128,16,128]{0,2,1:T(8,128)S(1)} %fusion.16, f32[16,8,128]{1,2,0:T(8,128)} %copy.75), kind=kLoop, calls=%fused_computation.18 | loop fusion | flops 16384 | bytes 196608 | tf_op jit(solution)/shard_map/add | solution.py:116
  87.7 5.1 %scatter-add.6 = f32[128,16,128]{0,2,1:T(8,128)S(1)} dynamic-update-slice(f32[128,16,128]{0,2,1:T(8,128)S(1)} %fusion.16, f32[8,16,128]{0,2,1:T(8,128)} %slice_add_fusion.3, s32[]{:T(128)} %constant.113.clone.1, s32[]{:T(128)} %constant.113.clone.1, s32[]{:T(128)} %constant.113.clone.1) | dynamic-update-slice | bytes 131076 | tf_op jit(solution)/shard_map/scatter-add | solution.py:116
  92.8 1.4 %copy.83 = f32[128,16,128]{2,1,0:T(8,128)} copy(f32[128,16,128]{0,2,1:T(8,128)S(1)} %scatter-add.6) | data formatting | bytes 2097152
  94.3 0.9 copy.84
  (44 shorter events, 0.6 us)
Async XLA Ops:
  7.2 39.2 %copy-start = (bf16[1,48,128,128]{3,2,1,0:T(8,128)(2,1)S(1)}, bf16[1,48,128,128]{3,2,1,0:T(8,128)(2,1)}, u32[]{:S(2)}) copy-start(bf16[1,48,128,128]{3,2,1,0:T(8,128)(2,1)} %param.20) | copy-start | bytes 4718596
  7.2 7.1 %copy-start.8 = (s32[1,48]{1,0:T(1,128)S(1)}, s32[1,48]{1,0:T(1,128)}, u32[]{:S(2)}) copy-start(s32[1,48]{1,0:T(1,128)} %param.21) | copy-start | bytes 580
  7.2 7.1 %copy-start.6 = (s32[1,48]{1,0:T(1,128)S(1)}, s32[1,48]{1,0:T(1,128)}, u32[]{:S(2)}) copy-start(s32[1,48]{1,0:T(1,128)} %param.22) | copy-start | bytes 580
  7.2 22.7 %copy-start.1 = (f32[48,16,128]{2,1,0:T(8,128)S(1)}, f32[48,16,128]{2,1,0:T(8,128)}, u32[]{:S(2)}) copy-start(f32[48,16,128]{2,1,0:T(8,128)} %param.16) | copy-start | bytes 1179652
  7.2 22.9 %copy-start.7 = (s32[16,1]{0,1:T(1,128)S(1)}, s32[16,1]{0,1:T(1,128)}, u32[]{:S(2)}) copy-start(s32[16,1]{0,1:T(1,128)} %param.19) | copy-start | bytes 196
  7.2 75.9 %reduce-scatter.2.cloned.1.call-start = ((), (), s32[]{:S(2)}) async-start(), calls=%async_computation.1 | async-start | bytes 655360 | tf_op jit(solution)/shard_map/reduce_scatter | solution.py:96
  10.1 64.1 %collective-permute-start = (f32[128,2,128]{0,1,2:T(2,128)}, f32[128,2,128]{0,1,2:T(2,128)}, u32[]{:S(2)}, u32[]{:S(2)}) collective-permute-start(f32[128,2,128]{0,1,2:T(2,128)} %get-tuple-element.37), channel_id=1, source_target_pairs={{0,4},{4,8},{8,12},{12,16},{16,20},{20,24},{24,28},{28,0},{1,5},{5... | collective-permute-start | bytes 393224 | tf_op jit(solution)/shard_map/ppermute | solution.py:15
  10.6 63.6 %collective-permute-start.1 = (f32[128,2,128]{0,1,2:T(2,128)}, f32[128,2,128]{0,1,2:T(2,128)}, u32[]{:S(2)}, u32[]{:S(2)}) collective-permute-start(f32[128,2,128]{0,1,2:T(2,128)} %get-tuple-element.38), channel_id=1, source_target_pairs={{4,0},{8,4},{12,8},{16,12},{20,16},{24,20},{28,24},{0,28},{5,1},{9... | collective-permute-start | bytes 393224 | tf_op jit(solution)/shard_map/ppermute | solution.py:18
  30.1 0.7 copy-start.2
  46.4 0.6 copy-start.5
  54.8 4.5 %collective-permute-start.4 = (f32[48,2,128]{2,0,1:T(8,128)S(1)}, f32[48,2,128]{2,0,1:T(8,128)}, u32[]{:S(2)}, u32[]{:S(2)}) collective-permute-start(f32[48,2,128]{2,0,1:T(8,128)S(1)} %get-tuple-element.42), channel_id=1, source_target_pairs={{0,4},{4,8},{8,12},{12,16},{16,20},{20,24},{24,28},{28,0},{1,5},{5... | collective-permute-start | bytes 147464 | tf_op jit(solution)/shard_map/ppermute | solution.py:15
  54.8 5.4 %collective-permute-start.5 = (f32[48,2,128]{2,0,1:T(8,128)}, f32[48,2,128]{2,0,1:T(8,128)}, u32[]{:S(2)}, u32[]{:S(2)}) collective-permute-start(f32[48,2,128]{2,0,1:T(8,128)} %get-tuple-element.41), channel_id=1, source_target_pairs={{4,0},{8,4},{12,8},{16,12},{20,16},{24,20},{28,24},{0,28},{5,1},{9... | collective-permute-start | bytes 147464 | tf_op jit(solution)/shard_map/ppermute | solution.py:18
  63.3 6.0 %collective-permute-start.6 = (f32[48,20,2]{0,1,2:T(8,128)S(1)}, f32[48,20,2]{0,1,2:T(8,128)S(1)}, u32[]{:S(2)}, u32[]{:S(2)}) collective-permute-start(f32[48,20,2]{0,1,2:T(8,128)S(1)} %copy.79), channel_id=1, source_target_pairs={{0,1},{1,2},{2,3},{3,0},{4,5},{5,6},{6,7},{7,4},{8,9},{9,10},{10,1... | collective-permute-start | bytes 23048 | tf_op jit(solution)/shard_map/ppermute | solution.py:15
  66.2 4.3 %collective-permute-start.7 = (f32[48,20,2]{0,1,2:T(8,128)S(1)}, f32[48,20,2]{0,1,2:T(8,128)S(1)}, u32[]{:S(2)}, u32[]{:S(2)}) collective-permute-start(f32[48,20,2]{0,1,2:T(8,128)S(1)} %copy.80), channel_id=1, source_target_pairs={{1,0},{2,1},{3,2},{0,3},{5,4},{6,5},{7,6},{4,7},{9,8},{10,9},{11,1... | collective-permute-start | bytes 23048 | tf_op jit(solution)/shard_map/ppermute | solution.py:18
  70.4 2.7 %copy-start.3 = (f32[48]{0:T(128)S(1)}, f32[48]{0:T(128)}, u32[]{:S(2)}) copy-start(f32[48]{0:T(128)} %param.18) | copy-start | bytes 580
  75.4 6.1 %collective-permute-start.2 = (f32[128,20,2]{0,1,2:T(8,128)S(1)}, f32[128,20,2]{0,1,2:T(8,128)S(1)}, u32[]{:S(2)}, u32[]{:S(2)}) collective-permute-start(f32[128,20,2]{0,1,2:T(8,128)S(1)} %get-tuple-element.35), channel_id=1, source_target_pairs={{0,1},{1,2},{2,3},{3,0},{4,5},{5,6},{6,7},{7,4},{8,9},{9,10},{10,1... | collective-permute-start | bytes 61448 | tf_op jit(solution)/shard_map/ppermute | solution.py:15
  76.7 4.9 %collective-permute-start.3 = (f32[128,20,2]{0,1,2:T(8,128)S(1)}, f32[128,20,2]{0,1,2:T(8,128)S(1)}, u32[]{:S(2)}, u32[]{:S(2)}) collective-permute-start(f32[128,20,2]{0,1,2:T(8,128)S(1)} %get-tuple-element.36), channel_id=1, source_target_pairs={{1,0},{2,1},{3,2},{0,3},{5,4},{6,5},{7,6},{4,7},{9,8},{10,9},{11,1... | collective-permute-start | bytes 61448 | tf_op jit(solution)/shard_map/ppermute | solution.py:18
  81.6 0.7 copy-start.4
Sparse Core Ops, SparseCore 0:
  53.4 22.3 reduce-scatter.1
where the time goes:
time: 103 us; the launch traced here: 102 us
  blocking collectives  28.6 us (28%)
  local copies, waits for them, and re-layouts  26.5 us (26%)
  between operations  15 us (15%)
  starting transfers between devices  14.4 us (14%)
  other arithmetic  9.11 us (9%)
  matrix products  4.66 us (5%)
  waiting for transfers between devices  3.77 us (4%)
    all_gather x1, blocking collectives, shards(): lax.all_gather(atm_source, 'tile', axis=1, tiled=True)  14.4 us
    all_gather x1, blocking collectives, shards(): lax.all_gather(ocean_source, 'tile', axis=1, tiled=True)  14.3 us
    ppermute x4, starting transfers between devices, padded_2(): lax.ppermute(lax.slice_in_dim(block, 0, width, axis=dim), axis, backward)  11 us
    unnamed x28, local copies, waits for them, and re-layouts  7.44 us
    scatter-add x1, local copies, waits for them, and re-layouts, shards(): atm_next = atm_stepped.at[:SURF].add(jnp.transpose(atm_force, (1, 0, 2)))  5.1 us
    ppermute x4, waiting for transfers between devices, padded_2(): lax.ppermute(lax.slice_in_dim(block, block.shape[dim] - width, None, axis...  3.67 us
    mul x4, other arithmetic, ghosts(): return padded * retain[None, :, None]  3.33 us
    ppermute x4, starting transfers between devices, padded_2(): lax.ppermute(lax.slice_in_dim(block, block.shape[dim] - width, None, axis...  3.33 us
  transfers between devices with their start and end apart: 9, of which 4 were waited for; matrix products, arithmetic and copies ran while one was open for 24% of the time, Pallas kernels for 0%

commit v1 on v0

--- a/solution.py
+++ b/solution.py
@@ -4,6 +4,22 @@
 from jax.sharding import PartitionSpec as P
 
 SURF = 8
+
+
+def gather_around(x, axis, dim):
+    ways, here, hop = (lax.axis_size(axis), lax.axis_index(axis), x.shape[dim])
+    shape = [n * ways if d == dim else n for d, n in enumerate(x.shape)]
+    full = lax.dynamic_update_slice_in_dim(jnp.zeros(shape, x.dtype), x, here * hop, axis=dim)
+    going_up = going_down = x
+    for far in range(1, ways // 2 + 1):
+        going_up = lax.ppermute(going_up, axis, [(d, (d + 1) % ways) for d in range(ways)])
+        full = lax.dynamic_update_slice_in_dim(full, going_up, (here - far) % ways * hop, axis=dim)
+        if 2 * far < ways:
+            going_down = lax.ppermute(going_down, axis, [(d, (d - 1) % ways) for d in range(ways)])
+            full = lax.dynamic_update_slice_in_dim(
+                full, going_down, (here + far) % ways * hop, axis=dim
+            )
+    return full
 
 
 def padded_2(block, sides, width):
@@ -57,7 +73,7 @@
     atm_source = atm_state[:SURF].astype(jnp.bfloat16)
     ocean_source = (ocean_state[:SURF] * wet_rows[None, :, None]).astype(jnp.bfloat16)
     atm_band, ocean_band = (
-        lax.all_gather(atm_source, "tile", axis=1, tiled=True),
+        gather_around(atm_source, "tile", 1),
         lax.all_gather(ocean_source, "tile", axis=1, tiled=True),
     )
     anchor = pair_src[0]

time: 103 us -> 106 us (1.029)
  blocking collectives: 28.6 us -> 13.4 us
  waiting for transfers between devices: 3.77 us -> 18.5 us
  other arithmetic: 9.11 us -> 12.7 us
  local copies, waits for them, and re-layouts: 26.5 us -> 28.8 us
  starting transfers between devices: 14.4 us -> 12.4 us
    all_gather x1 -> x0, blocking collectives: 14.4 us -> none  [shards(): lax.all_gather(atm_source, 'tile', axis=1, tiled=True)]
    reduce_scatter x1, waiting for transfers between devices: 0.02 us -> 11.9 us  [shards(): lax.psum_scatter(jnp.dot(ahead_hot, ahead_flat, precision=lax.Precision.H...]
    ppermute x4, starting transfers between devices: 11 us -> 5.57 us  [padded_2(): lax.ppermute(lax.slice_in_dim(block, 0, width, axis=dim), axis, backward)]
    ppermute x0 -> x3, starting transfers between devices: none -> 5.19 us  [the longest x2 3.1 us: gather_around(): lax.ppermute(going_up, axis, [(d, (d + 1) % ways) for d in range(ways)])]
    dynamic_update_slice x0 -> x4, local copies, waits for them, and re-layouts: none -> 4.72 us  [the longest x2 2.73 us: gather_around(): lax.dynamic_update_slice_in_dim(full, going_up, (here - far) % ways * hop...]
    ppermute x4, waiting for transfers between devices: 3.67 us -> 5.68 us  [padded_2(): lax.ppermute(lax.slice_in_dim(block, block.shape[dim] - width, None, axis...]
    ppermute x4, starting transfers between devices: 3.33 us -> 1.65 us  [padded_2(): lax.ppermute(lax.slice_in_dim(block, block.shape[dim] - width, None, axis...]
    gather x1, local copies, waits for them, and re-layouts: 0.61 us -> 2.27 us  [shards(): jnp.take(atm_band, anchor, axis=1)]
  transfers between devices with their start and end apart: 9 -> 12, of which waited for: 4 -> 5; matrix products, arithmetic and copies ran while one was open for 24% -> 30% of each run, Pallas kernels for 0% -> 0%
where the time goes in v1:
time: 106 us
  local copies, waits for them, and re-layouts  28.8 us (27%)
  waiting for transfers between devices  18.5 us (17%)
  between operations  15 us (14%)
  blocking collectives  13.4 us (13%)
  other arithmetic  12.7 us (12%)
  starting transfers between devices  12.4 us (12%)
  matrix products  4.72 us (4%)
    all_gather x1, blocking collectives, shards(): lax.all_gather(ocean_source, 'tile', axis=1, tiled=True)  13.4 us
    reduce_scatter x1, waiting for transfers between devices, shards(): lax.psum_scatter(jnp.dot(ahead_hot, ahead_flat, precision=lax.Precision.H...  11.9 us
    unnamed x45, local copies, waits for them, and re-layouts  5.8 us
    ppermute x4, waiting for transfers between devices, padded_2(): lax.ppermute(lax.slice_in_dim(block, block.shape[dim] - width, None, axis...  5.68 us
    ppermute x4, starting transfers between devices, padded_2(): lax.ppermute(lax.slice_in_dim(block, 0, width, axis=dim), axis, backward)  5.57 us
    scatter-add x1, local copies, waits for them, and re-layouts, shards(): atm_next = atm_stepped.at[:SURF].add(jnp.transpose(atm_force, (1, 0, 2)))  5.1 us
    mul x4, other arithmetic, ghosts(): return padded * retain[None, :, None]  3.34 us
    slice x4, local copies, waits for them, and re-layouts, padded_2(): lax.slice_in_dim(block, block.shape[dim] - width, None, axis=dim)  3.15 us
  transfers between devices with their start and end apart: 12, of which 5 were waited for; matrix products, arithmetic and copies ran while one was open for 30% of the time, Pallas kernels for 0%

profile of v1, /device:TPU:0, one launch (start us, length us, event | category | flops | bytes accessed | tf_op | source)
XLA Modules:
  0.0 105.6 jit_solution(17020898010968369525)
XLA Ops:
  7.2 1.0 slice.198
  8.2 0.7 broadcast_in_dim.14
  8.9 0.6 constant_dynamic-update-slice_fusion.6
  9.5 3.1 %collective-permute-start.4 = (bf16[8,16,128]{2,0,1:T(8,128)(2,1)}, bf16[8,16,128]{2,0,1:T(8,128)(2,1)}, u32[]{:S(2)}, u32[]{:S(2)}) collective-permute-start(bf16[8,16,128]{2,0,1:T(8,128)(2,1)} %get-tuple-element.36), channel_id=1, source_target_pairs={{0,1},{1,2},{2,3},{3,0},{4,5},{5,6},{6,7},{7,4},{8,9},{9,10},{10,1... | collective-permute-start | bytes 98312 | tf_op jit(solution)/shard_map/ppermute | solution.py:15
  12.6 2.1 %collective-permute-start.5 = (bf16[8,16,128]{2,0,1:T(8,128)(2,1)}, bf16[8,16,128]{2,0,1:T(8,128)(2,1)}, u32[]{:S(2)}, u32[]{:S(2)}) collective-permute-start(bf16[8,16,128]{2,0,1:T(8,128)(2,1)} %get-tuple-element.36), channel_id=1, source_target_pairs={{0,3},{1,0},{2,1},{3,2},{4,7},{5,4},{6,5},{7,6},{8,11},{9,8},{10,9... | collective-permute-start | bytes 98312 | tf_op jit(solution)/shard_map/ppermute | solution.py:18
  14.7 1.8 %copy.66 = f32[128,16,128]{0,1,2:T(8,128)S(1)} copy(f32[128,16,128]{2,1,0:T(8,128)} %param.15) | data formatting | bytes 2097152 | tf_op args[0]
  16.5 0.8 fusion.48
  17.3 1.6 %collective-permute-start.1 = (f32[128,2,128]{0,1,2:T(2,128)}, f32[128,2,128]{0,1,2:T(2,128)}, u32[]{:S(2)}, u32[]{:S(2)}) collective-permute-start(f32[128,2,128]{0,1,2:T(2,128)} %get-tuple-element.40), channel_id=1, source_target_pairs={{4,0},{8,4},{12,8},{16,12},{20,16},{24,20},{28,24},{0,28},{5,1},{9... | collective-permute-start | bytes 393224 | tf_op jit(solution)/shard_map/ppermute | solution.py:34
  19.1 0.6 fusion.50
  19.9 0.6 compare_and_fusion.1
  20.5 0.6 pad_clamp_fusion.1
  21.8 0.5 fusion.43
  22.3 0.5 copy-done.6
  22.8 13.4 %all_gather.3 = bf16[8,64,128]{2,0,1:T(8,128)(2,1)S(1)} all-gather(bf16[8,16,128]{2,0,1:T(8,128)(2,1)S(1)} %fusion.36), channel_id=1, replica_groups=mesh['comp'=8,'tile'=4] {'tile'}, dimensions={1}, use_global_device_ids=true | all-gather | bytes 163840 | tf_op jit(solution)/shard_map/all_gather | solution.py:77
  36.2 1.2 %fusion.44 = s32[48]{0:T(128)} fusion(s32[1,48]{1,0:T(1,128)} %param.21, s32[]{:T(128)} %bitcast.51), kind=kLoop, calls=%fused_computation.95 | loop fusion | flops 1104 | bytes 388 | tf_op jit(solution)/shard_map/eq | solution.py:111
  37.4 0.6 not_convert_fusion.1
  38.0 0.6 gather_fusion.1
  38.6 1.6 %fusion.11 = f32[48,8,128]{2,1,0:T(8,128)} fusion(bf16[1,48,128,128]{3,2,1,0:T(8,128)(2,1)S(1)} %copy-done, bf16[48,8,128]{2,1,0:T(8,128)(2,1)S(1)} %gather_fusion.1, f32[48]{0:T(128)S(1)} %compare_convert_fusion, pred[48]{0:T(512)(128)(4,1)S(1)} %compare_and_fusion), kind=kOutput, calls=%fused_computation.17 | convolution fusion | flops 12681216 | bytes 1868016 | tf_op jit(solution)/shard_map/fps,pts->pft/dot_general | solution.py:94
  40.3 0.5 not_convert_fusion
  40.8 1.4 %constant_dynamic-update-slice_fusion.5 = bf16[8,64,128]{2,0,1:T(8,128)(2,1)} fusion(bf16[8,64,128]{2,0,1:T(8,128)(2,1)} %get-tuple-element.35, bf16[8,16,128]{2,0,1:T(8,128)(2,1)} %collective-permute-done.4, s32[]{:T(128)S(6)} %select_n.69), kind=kLoop, calls=%fused_computation.82 | loop fusion | bytes 65540 | tf_op jit(solution)/shard_map/dynamic_update_slice | solution.py:16
  42.3 0.6 collective-permute-done.8
  42.9 1.1 %fusion.49 = (f32[48,20,2]{2,0,1:T(8,128)}, f32[48,20,2]{2,0,1:T(8,128)}) fusion(f32[48,20,128]{2,0,1:T(8,128)S(1)} %constant_dynamic-update-slice_fusion), kind=kLoop, calls=%fused_computation.101 | loop fusion | bytes 30720 | tf_op jit(solution)/shard_map/slice | solution.py:32
  44.0 1.3 %copy.79 = f32[48,20,2]{0,1,2:T(8,128)S(1)} copy(f32[48,20,2]{2,0,1:T(8,128)} %get-tuple-element.42) | data formatting | bytes 15360 | tf_op jit(solution)/shard_map/slice | solution.py:34
  45.2 3.3 %collective-permute-start.10 = (f32[48,20,2]{0,1,2:T(8,128)S(1)}, f32[48,20,2]{0,1,2:T(8,128)S(1)}, u32[]{:S(2)}, u32[]{:S(2)}) collective-permute-start(f32[48,20,2]{0,1,2:T(8,128)S(1)} %copy.79), channel_id=1, source_target_pairs={{1,0},{2,1},{3,2},{0,3},{5,4},{6,5},{7,6},{4,7},{9,8},{10,9},{11,1... | collective-permute-start | bytes 23048 | tf_op jit(solution)/shard_map/ppermute | solution.py:34
  48.6 1.3 %copy.78 = f32[48,20,2]{0,1,2:T(8,128)S(1)} copy(f32[48,20,2]{2,0,1:T(8,128)} %get-tuple-element.41) | data formatting | bytes 15360 | tf_op jit(solution)/shard_map/slice | solution.py:32
  49.9 1.4 %constant_dynamic-update-slice_fusion.4 = bf16[8,64,128]{2,0,1:T(8,128)(2,1)} fusion(bf16[8,64,128]{2,0,1:T(8,128)(2,1)} %constant_dynamic-update-slice_fusion.5, bf16[8,16,128]{2,0,1:T(8,128)(2,1)} %collective-permute-done.5, s32[]{:T(128)S(6)} %select_n.71), kind=kLoop, calls=%fused_computation.81 | loop fusion | bytes 65540 | tf_op jit(solution)/shard_map/dynamic_update_slice | solution.py:19
  51.3 1.0 copy.81
  52.3 3.2 %collective-permute-done.9 = f32[48,20,2]{0,1,2:T(8,128)S(1)} collective-permute-done((f32[48,20,2]{0,1,2:T(8,128)S(1)}, f32[48,20,2]{0,1,2:T(8,128)S(1)}, u32[]{:S(2)}, u32[]{:S(2)}) %collective-permute-start.9) | collective-permute-done | bytes 7712 | tf_op jit(solution)/shard_map/ppermute | solution.py:31
  55.5 1.0 copy.80
  56.5 1.6 %maximum_multiply_fusion.1 = f32[48,20,132]{2,0,1:T(8,128)S(1)} fusion(f32[48,20,2]{2,0,1:T(8,128)} %copy.81, f32[48,20,128]{2,0,1:T(8,128)S(1)} %constant_dynamic-update-slice_fusion, f32[48,20,2]{2,0,1:T(8,128)} %copy.80, f32[20]{0:T(128)S(1)} %copy-done.11), kind=kLoop, calls=%fused_computation.25 | loop fusion | flops 380160 | bytes 1013840 | tf_op jit(solution)/shard_map/mul | solution.py:54
  58.2 1.0 fusion.20
  59.2 1.4 %constant_dynamic-update-slice_fusion.3 = bf16[8,64,128]{2,0,1:T(8,128)(2,1)} fusion(bf16[8,64,128]{2,0,1:T(8,128)(2,1)} %constant_dynamic-update-slice_fusion.4, bf16[8,16,128]{2,0,1:T(8,128)(2,1)} %collective-permute-done.6, s32[]{:T(128)S(6)} %select_n.73), kind=kLoop, calls=%fused_computation.80 | loop fusion | bytes 65540 | tf_op jit(solution)/shard_map/dynamic_update_slice | solution.py:16
  60.6 2.3 %gather_fusion = bf16[48,8,128]{2,1,0:T(8,128)(2,1)} fusion(bf16[8,64,128]{2,0,1:T(8,128)(2,1)} %constant_dynamic-update-slice_fusion.3, s32[1024]{0:T(1024)} %pad_clamp_fusion.1), kind=kCustom, calls=%fused_computation.clone | custom fusion | bytes 196800 | tf_op jit(solution)/shard_map/jit(_take)/gather | solution.py:87
  62.9 1.5 %fusion.8 = f32[48,8,128]{2,1,0:T(8,128)S(1)} fusion(bf16[1,48,128,128]{3,2,1,0:T(8,128)(2,1)S(1)} %copy-done, bf16[48,8,128]{2,1,0:T(8,128)(2,1)} %gather_fusion, f32[48]{0:T(128)S(1)} %copy-done.10, pred[48]{0:T(512)(128)(4,1)S(1)} %copy-done.12), kind=kOutput, calls=%fused_computation.16 | convolution fusion | flops 12681216 | bytes 1868016 | tf_op jit(solution)/shard_map/fpt,pts->pfs/dot_general | solution.py:85
  64.8 1.2 %convolution_add_fusion = f32[128,1024]{1,0:T(8,128)} fusion(f32[128,1024]{1,0:T(8,128)S(1)} %fusion.26, f32[6,8,8,128]{3,2,1,0:T(8,128)S(1)} %bitcast.52, s32[48]{0:T(128)S(1)} %copy-done.14), kind=kOutput, calls=%fused_computation.15 | convolution fusion | flops 75634688 | bytes 1245376 | tf_op jit(solution)/shard_map/dot_general | solution.py:119
  66.0 1.2 %pad_maximum_fusion = f32[128,20,128]{0,1,2:T(8,128)S(1)} fusion(f32[128,2,128]{0,1,2:T(2,128)} %collective-permute-done.1, f32[128,16,128]{0,1,2:T(8,128)S(1)} %copy.66, f32[128,2,128]{0,1,2:T(2,128)} %collective-permute-done), kind=kLoop, calls=%fused_computation.2 | loop fusion | flops 655360 | bytes 2621440 | tf_op jit(solution)/shard_map/concatenate | solution.py:35
  67.3 0.6 collective-permute-start.3
  67.9 1.4 %collective-permute-start.2 = (f32[128,20,2]{0,1,2:T(8,128)S(1)}, f32[128,20,2]{0,1,2:T(8,128)S(1)}, u32[]{:S(2)}, u32[]{:S(2)}) collective-permute-start(f32[128,20,2]{0,1,2:T(8,128)S(1)} %get-tuple-element.37), channel_id=1, source_target_pairs={{0,1},{1,2},{2,3},{3,0},{4,5},{5,6},{6,7},{7,4},{8,9},{9,10},{10,1... | collective-permute-start | bytes 61448 | tf_op jit(solution)/shard_map/ppermute | solution.py:31
  69.3 1.2 %fusion.23 = f32[48,16,128]{2,0,1:T(8,128)} fusion(f32[48,18,130]{2,0,1:T(8,128)S(1)} %fusion.20, f32[48]{0:T(128)S(1)} %copy-done.4), kind=kLoop, calls=%fused_computation.36 | loop fusion | flops 688128 | bytes 2359488 | tf_op jit(solution)/shard_map/add | solution.py:44
  71.2 2.5 %collective-permute-done.2 = f32[128,20,2]{0,1,2:T(8,128)S(1)} collective-permute-done((f32[128,20,2]{0,1,2:T(8,128)S(1)}, f32[128,20,2]{0,1,2:T(8,128)S(1)}, u32[]{:S(2)}, u32[]{:S(2)}) %collective-permute-start.2) | collective-permute-done | bytes 20512 | tf_op jit(solution)/shard_map/ppermute | solution.py:31
  73.8 0.5 fusion.7
  74.8 11.9 %reduce-scatter.2.cloned.1.call-done = f32[32,1024]{1,0:T(8,128)} async-done(((f32[128,1024]{1,0:T(8,128)}), f32[32,1024]{1,0:T(8,128)}) %reduce-scatter.2.cloned.1.call-update) | async-done | bytes 131088 | tf_op jit(solution)/shard_map/reduce_scatter | solution.py:112
  86.7 0.9 slice_bitcast_fusion
  87.6 1.3 %copy.74 = f32[16,8,128]{1,2,0:T(8,128)} copy(f32[16,8,128]{2,1,0:T(8,128)S(1)} %bitcast.54) | data formatting | bytes 131072 | tf_op jit(solution)/shard_map/reshape | solution.py:126
  88.9 2.3 %slice_add_fusion.3 = f32[8,16,128]{0,2,1:T(8,128)} fusion(f32[128,16,128]{0,2,1:T(8,128)S(1)} %fusion.16, f32[16,8,128]{1,2,0:T(8,128)} %copy.74), kind=kLoop, calls=%fused_computation.18 | loop fusion | flops 16384 | bytes 196608 | tf_op jit(solution)/shard_map/add | solution.py:132
  91.2 5.1 %scatter-add.6 = f32[128,16,128]{0,2,1:T(8,128)S(1)} dynamic-update-slice(f32[128,16,128]{0,2,1:T(8,128)S(1)} %fusion.16, f32[8,16,128]{0,2,1:T(8,128)} %slice_add_fusion.3, s32[]{:T(128)} %constant.139.clone.1, s32[]{:T(128)} %constant.139.clone.1, s32[]{:T(128)} %constant.139.clone.1) | dynamic-update-slice | bytes 131076 | tf_op jit(solution)/shard_map/scatter-add | solution.py:132
  96.4 1.4 %copy.82 = f32[128,16,128]{2,1,0:T(8,128)} copy(f32[128,16,128]{0,2,1:T(8,128)S(1)} %scatter-add.6) | data formatting | bytes 2097152
  97.9 0.9 copy.83
  (71 shorter events, 2.4 us)
Async XLA Ops:
  7.2 31.5 %copy-start = (bf16[1,48,128,128]{3,2,1,0:T(8,128)(2,1)S(1)}, bf16[1,48,128,128]{3,2,1,0:T(8,128)(2,1)}, u32[]{:S(2)}) copy-start(bf16[1,48,128,128]{3,2,1,0:T(8,128)(2,1)} %param.20) | copy-start | bytes 4718596
  7.2 79.5 %reduce-scatter.2.cloned.1.call-start = ((), (), s32[]{:S(2)}) async-start(), calls=%async_computation.1 | async-start | bytes 655360 | tf_op jit(solution)/shard_map/reduce_scatter | solution.py:112
  8.9 10.1 %copy-start.2 = (f32[48,16,128]{2,1,0:T(8,128)S(1)}, f32[48,16,128]{2,1,0:T(8,128)}, u32[]{:S(2)}) copy-start(f32[48,16,128]{2,1,0:T(8,128)} %param.16) | copy-start | bytes 1179652
  9.5 10.4 %copy-start.17 = (s32[1,48]{1,0:T(1,128)S(1)}, s32[1,48]{1,0:T(1,128)}, u32[]{:S(2)}) copy-start(s32[1,48]{1,0:T(1,128)} %param.21) | copy-start | bytes 580
  9.5 11.0 %copy-start.15 = (s32[1,48]{1,0:T(1,128)S(1)}, s32[1,48]{1,0:T(1,128)}, u32[]{:S(2)}) copy-start(s32[1,48]{1,0:T(1,128)} %param.22) | copy-start | bytes 580
  9.5 12.8 %copy-start.16 = (s32[16,1]{0,1:T(1,128)S(1)}, s32[16,1]{0,1:T(1,128)}, u32[]{:S(2)}) copy-start(s32[16,1]{0,1:T(1,128)} %param.19) | copy-start | bytes 196
  9.5 31.3 %collective-permute-start.4 = (bf16[8,16,128]{2,0,1:T(8,128)(2,1)}, bf16[8,16,128]{2,0,1:T(8,128)(2,1)}, u32[]{:S(2)}, u32[]{:S(2)}) collective-permute-start(bf16[8,16,128]{2,0,1:T(8,128)(2,1)} %get-tuple-element.36), channel_id=1, source_target_pairs={{0,1},{1,2},{2,3},{3,0},{4,5},{5,6},{6,7},{7,4},{8,9},{9,10},{10,1... | collective-permute-start | bytes 98312 | tf_op jit(solution)/shard_map/ppermute | solution.py:15
  12.6 37.2 %collective-permute-start.5 = (bf16[8,16,128]{2,0,1:T(8,128)(2,1)}, bf16[8,16,128]{2,0,1:T(8,128)(2,1)}, u32[]{:S(2)}, u32[]{:S(2)}) collective-permute-start(bf16[8,16,128]{2,0,1:T(8,128)(2,1)} %get-tuple-element.36), channel_id=1, source_target_pairs={{0,3},{1,0},{2,1},{3,2},{4,7},{5,4},{6,5},{7,6},{8,11},{9,8},{10,9... | collective-permute-start | bytes 98312 | tf_op jit(solution)/shard_map/ppermute | solution.py:18
  17.3 48.7 %collective-permute-start.1 = (f32[128,2,128]{0,1,2:T(2,128)}, f32[128,2,128]{0,1,2:T(2,128)}, u32[]{:S(2)}, u32[]{:S(2)}) collective-permute-start(f32[128,2,128]{0,1,2:T(2,128)} %get-tuple-element.40), channel_id=1, source_target_pairs={{4,0},{8,4},{12,8},{16,12},{20,16},{24,20},{28,24},{0,28},{5,1},{9... | collective-permute-start | bytes 393224 | tf_op jit(solution)/shard_map/ppermute | solution.py:34
  19.0 47.1 %collective-permute-start = (f32[128,2,128]{0,1,2:T(2,128)}, f32[128,2,128]{0,1,2:T(2,128)}, u32[]{:S(2)}, u32[]{:S(2)}) collective-permute-start(f32[128,2,128]{0,1,2:T(2,128)} %get-tuple-element.39), channel_id=1, source_target_pairs={{0,4},{4,8},{8,12},{12,16},{16,20},{20,24},{24,28},{28,0},{1,5},{5... | collective-permute-start | bytes 393224 | tf_op jit(solution)/shard_map/ppermute | solution.py:31
  19.7 22.5 %collective-permute-start.7 = (f32[48,2,128]{2,0,1:T(8,128)S(1)}, f32[48,2,128]{2,0,1:T(8,128)S(1)}, u32[]{:S(2)}, u32[]{:S(2)}) collective-permute-start(f32[48,2,128]{2,0,1:T(8,128)S(1)} %get-tuple-element.44), channel_id=1, source_target_pairs={{0,4},{4,8},{8,12},{12,16},{16,20},{20,24},{24,28},{28,0},{1,5},{5... | collective-permute-start | bytes 147464 | tf_op jit(solution)/shard_map/ppermute | solution.py:31
  21.7 20.5 %copy-start.9 = (f32[48]{0:T(128)}, f32[48]{0:T(128)S(1)}, u32[]{:S(2)}) copy-start(f32[48]{0:T(128)S(1)} %compare_convert_fusion) | copy-start | bytes 580
  22.3 0.6 copy-start.6
  40.8 2.1 %collective-permute-start.8 = (f32[48,2,128]{2,0,1:T(8,128)}, f32[48,2,128]{2,0,1:T(8,128)S(1)}, u32[]{:S(2)}, u32[]{:S(2)}) collective-permute-start(f32[48,2,128]{2,0,1:T(8,128)} %get-tuple-element.43), channel_id=1, source_target_pairs={{4,0},{8,4},{12,8},{16,12},{20,16},{24,20},{28,24},{0,28},{5,1},{9... | collective-permute-start | bytes 147464 | tf_op jit(solution)/shard_map/ppermute | solution.py:34
  42.2 17.0 %collective-permute-start.6 = (bf16[8,16,128]{2,0,1:T(8,128)(2,1)}, bf16[8,16,128]{2,0,1:T(8,128)(2,1)}, u32[]{:S(2)}, u32[]{:S(2)}) collective-permute-start(bf16[8,16,128]{2,0,1:T(8,128)(2,1)} %collective-permute-done.4), channel_id=1, source_target_pairs={{0,1},{1,2},{2,3},{3,0},{4,5},{5,6},{6,7},{7,4},{8,9},{9,10},{10,1... | collective-permute-start | bytes 98312 | tf_op jit(solution)/shard_map/ppermute | solution.py:15
  44.0 12.5 %copy-start.11 = (f32[20]{0:T(128)S(1)}, f32[20]{0:T(128)}, u32[]{:S(2)}) copy-start(f32[20]{0:T(128)} %not_convert_fusion.1) | copy-start | bytes 244
  45.2 6.0 %collective-permute-start.10 = (f32[48,20,2]{0,1,2:T(8,128)S(1)}, f32[48,20,2]{0,1,2:T(8,128)S(1)}, u32[]{:S(2)}, u32[]{:S(2)}) collective-permute-start(f32[48,20,2]{0,1,2:T(8,128)S(1)} %copy.79), channel_id=1, source_target_pairs={{1,0},{2,1},{3,2},{0,3},{5,4},{6,5},{7,6},{4,7},{9,8},{10,9},{11,1... | collective-permute-start | bytes 23048 | tf_op jit(solution)/shard_map/ppermute | solution.py:34
  49.8 5.7 %collective-permute-start.9 = (f32[48,20,2]{0,1,2:T(8,128)S(1)}, f32[48,20,2]{0,1,2:T(8,128)S(1)}, u32[]{:S(2)}, u32[]{:S(2)}) collective-permute-start(f32[48,20,2]{0,1,2:T(8,128)S(1)} %copy.78), channel_id=1, source_target_pairs={{0,1},{1,2},{2,3},{3,0},{4,5},{5,6},{6,7},{7,4},{8,9},{9,10},{10,1... | collective-permute-start | bytes 23048 | tf_op jit(solution)/shard_map/ppermute | solution.py:31
  52.3 5.9 %copy-start.4 = (f32[48]{0:T(128)S(1)}, f32[48]{0:T(128)}, u32[]{:S(2)}) copy-start(f32[48]{0:T(128)} %param.18) | copy-start | bytes 580
  52.3 5.9 %copy-start.8 = (f32[18]{0:T(128)S(1)}, f32[18]{0:T(128)}, u32[]{:S(2)}) copy-start(f32[18]{0:T(128)} %not_convert_fusion) | copy-start | bytes 220
  58.2 4.7 %copy-start.10 = (f32[48]{0:T(128)S(1)}, f32[48]{0:T(128)}, u32[]{:S(2)}) copy-start(f32[48]{0:T(128)} %copy-done.9) | copy-start | bytes 580
  58.2 4.7 %copy-start.12 = (pred[48]{0:T(512)(128)(4,1)S(1)}, pred[48]{0:T(512)(128)(4,1)}, u32[]{:S(2)}) copy-start(pred[48]{0:T(512)(128)(4,1)} %compare_and_fusion.1) | copy-start | bytes 148
  59.2 5.2 %copy-start.13 = (s32[48]{0:T(128)S(1)}, s32[48]{0:T(128)}, u32[]{:S(2)}) copy-start(s32[48]{0:T(128)} %fusion.43) | copy-start | bytes 580
  60.6 4.2 %copy-start.14 = (s32[48]{0:T(128)S(1)}, s32[48]{0:T(128)}, u32[]{:S(2)}) copy-start(s32[48]{0:T(128)} %fusion.44) | copy-start | bytes 580
  62.9 1.9 %copy-start.3 = (f32[48,8,128]{2,1,0:T(8,128)S(1)}, f32[48,8,128]{2,1,0:T(8,128)}, u32[]{:S(2)}) copy-start(f32[48,8,128]{2,1,0:T(8,128)} %fusion.11) | copy-start | bytes 589828
  67.3 3.9 %collective-permute-start.3 = (f32[128,20,2]{0,1,2:T(8,128)S(1)}, f32[128,20,2]{0,1,2:T(8,128)S(1)}, u32[]{:S(2)}, u32[]{:S(2)}) collective-permute-start(f32[128,20,2]{0,1,2:T(8,128)S(1)} %get-tuple-element.38), channel_id=1, source_target_pairs={{1,0},{2,1},{3,2},{0,3},{5,4},{6,5},{7,6},{4,7},{9,8},{10,9},{11,1... | collective-permute-start | bytes 61448 | tf_op jit(solution)/shard_map/ppermute | solution.py:34
  67.9 5.7 %collective-permute-start.2 = (f32[128,20,2]{0,1,2:T(8,128)S(1)}, f32[128,20,2]{0,1,2:T(8,128)S(1)}, u32[]{:S(2)}, u32[]{:S(2)}) collective-permute-start(f32[128,20,2]{0,1,2:T(8,128)S(1)} %get-tuple-element.37), channel_id=1, source_target_pairs={{0,1},{1,2},{2,3},{3,0},{4,5},{5,6},{6,7},{7,4},{8,9},{9,10},{10,1... | collective-permute-start | bytes 61448 | tf_op jit(solution)/shard_map/ppermute | solution.py:31
  71.2 2.7 %copy-start.5 = (f32[128]{0:T(128)S(1)}, f32[128]{0:T(128)}, u32[]{:S(2)}) copy-start(f32[128]{0:T(128)} %param.17) | copy-start | bytes 1540
  96.3 1.4 %copy-start.1 = (f32[48,16,128]{2,0,1:T(8,128)S(1)}, f32[48,16,128]{2,0,1:T(8,128)}, u32[]{:S(2)}) copy-start(f32[48,16,128]{2,0,1:T(8,128)} %fusion.23) | copy-start | bytes 1179652
  96.3 1.4 %copy-start.7 = (f32[16]{0:T(128)S(1)}, f32[16]{0:T(128)}, u32[]{:S(2)}) copy-start(f32[16]{0:T(128)} %copy-done.6) | copy-start | bytes 196
Sparse Core Ops, SparseCore 0:
  66.1 20.4 reduce-scatter.1
